TPU v7x, 256 devices: a whole 4x4x8 slice. The times are simulated.
256 devices in a mesh: gx: 8 (over y, core), gy: 16 (over x_hi, z), pa: 2 (over x_lo).
Axes of the slice: x: 4 (x_hi: 2, x_lo: 2; x = x_hi * 2 + x_lo), y: 4, z: 8, core: 2. Of those that a mesh axis runs over, the one named last changes fastest.
Arguments:
- volume: bfloat16 [4, 4096, 4096], P('pa', 'gx', 'gy'), may hold values from -6 to 6
- view_slopes: int32 [2, 16], replicated, may hold values from -14 to 14, as said below
- measured_x: float32 [16, 4, 4096], P(None, 'pa', 'gy'), may hold values from -6 to 6
- measured_y: float32 [16, 4, 4096], P(None, 'pa', 'gx'), may hold values from -6 to 6
Outputs:
- gradient: float32 [4, 4096, 4096], P('pa', 'gx', 'gy')
- residual_x: float32 [16, 4, 4096], P(None, 'pa', 'gy')
- residual_y: float32 [16, 4, 4096], P(None, 'pa', 'gx')
Inputs may be any that keep to these rules, and one draw needn't show every extreme that they name: `view_slopes`: row 0 holds the near-x slopes in units of 1/512, row 1 the near-y slopes in units of 1/256; in each row both 14 and its negative occur.
All inputs are finite; a program needn't handle non-finite values.
Results may differ from a plain program's by a relative error of at most 0.0025.
Values may be sent and summed in bfloat16 or wider, within the bound.
No kernel may reach another device: no remote copies, remote signals or barrier semaphores. Data moves between devices by JAX's collectives and lax.ppermute only.
A program may use at most 128 MiB of HBM per device.

v0:
```python
import jax
import jax.numpy as jnp
from jax import lax
from jax.sharding import PartitionSpec as P

SHEAR = 14


def padded_2(value, sides, width):
    for axis, dim in sides:
        size, length = (lax.axis_size(axis), value.shape[dim])
        up = [(i, (i + 1) % size) for i in range(size - 1)]
        down = [(j, i) for i, j in up]
        last = lax.slice_in_dim(value, length - width, length, axis=dim)
        leading = lax.slice_in_dim(value, 0, width, axis=dim)
        before = lax.ppermute(last, axis, up)
        after = lax.ppermute(leading, axis, down)
        value = jnp.concatenate([before, value, after], axis=dim)
    return value


def lane_round(value):
    return -(-value // 128) * 128


def shear_table(slopes, positions, cells, shift_levels):
    product = slopes[:, None] * positions[None, :]
    shifts = jnp.floor_divide(product, cells)
    fraction = (product - shifts * cells).astype(jnp.float32) / cells
    lowest = jnp.min(shifts, axis=1)
    offsets = shifts - lowest[:, None]
    levels = jnp.arange(shift_levels, dtype=jnp.int32)
    lower = (1.0 - fraction).astype(jnp.bfloat16)
    upper = fraction.astype(jnp.bfloat16)
    nothing = jnp.zeros((), jnp.bfloat16)
    table = jnp.where(levels[None, :, None] == offsets[:, None, :], lower[:, None, :], nothing)
    table = table + jnp.where(
        levels[None, :, None] == offsets[:, None, :] + 1, upper[:, None, :], nothing
    )
    return (table, lowest)


def shear_sum(summands, lowest, leading, number, pad_cells):
    planes, shift_levels, length = summands.shape
    natural_row = length + 2 * pad_cells
    right_pad = pad_cells + lane_round(natural_row + 1) - (natural_row + 1)
    row_length = length + pad_cells + right_pad
    padded = jnp.pad(summands, ((0, 0), (0, 0), (pad_cells, right_pad)))
    flattened = jnp.pad(
        padded.reshape(planes, shift_levels * row_length), ((0, 0), (0, shift_levels))
    )
    skewed = jnp.sum(flattened.reshape(planes, shift_levels, row_length + 1), axis=1)
    return lax.dynamic_slice_in_dim(skewed, leading + lowest + pad_cells, number, 1)


def spread(values, lowest, leading, number, pad_cells, shift_levels):
    planes, length = values.shape
    natural_row = length + 2 * pad_cells
    right_pad = pad_cells + lane_round(natural_row - 1) - (natural_row - 1)
    row_length = length + pad_cells + right_pad
    padded = jnp.pad(values, ((0, 0), (pad_cells, right_pad)))
    repeated = jnp.broadcast_to(padded[:, None, :], (planes, shift_levels, row_length))
    repeated = repeated.reshape(planes, shift_levels * row_length)
    skewed = repeated[:, : shift_levels * (row_length - 1)].reshape(
        planes, shift_levels, row_length - 1
    )
    return lax.dynamic_slice_in_dim(skewed, leading - lowest + pad_cells, number, 2)


def sheared_views(summands, lowest, leading, number, pad_cells):
    return jax.vmap(lambda pieces, low: shear_sum(pieces, low, leading, number, pad_cells))(
        summands, lowest
    )


def spread_views(values, lowest, leading, number, pad_cells, shift_levels):
    return jax.vmap(
        lambda pieces, low: spread(pieces, low, leading, number, pad_cells, shift_levels)
    )(values, lowest)


def fold_edges(inner, outer, ghost_width, length, dim):
    lead_pads = [(0, 0)] * inner.ndim
    tail_pads = [(0, 0)] * inner.ndim
    lead_pads[dim] = (0, length - ghost_width)
    tail_pads[dim] = (length - ghost_width, 0)
    head = lax.slice_in_dim(outer, 0, ghost_width, 1, dim)
    tail = lax.slice_in_dim(outer, length + 3 * ghost_width, length + 4 * ghost_width, 1, dim)
    return inner + jnp.pad(head, lead_pads) + jnp.pad(tail, tail_pads)


def on_device(volume, view_slopes, measured_x, measured_y):
    planes, cells_x, cells_y = volume.shape
    count_x = lax.axis_size("gx")
    count_y = lax.axis_size("gy")
    ghost_width = SHEAR * max(count_x, count_y) // 2 + 2
    shift_levels = SHEAR + 2
    pad_cells = 2 * ghost_width + shift_levels
    positions_x = (
        lax.axis_index("gx") * cells_x
        + jnp.arange(cells_x, dtype=jnp.int32)
        - cells_x * count_x // 2
    )
    positions_y = (
        lax.axis_index("gy") * cells_y
        + jnp.arange(cells_y, dtype=jnp.int32)
        - cells_y * count_y // 2
    )
    table_x, lowest_x = shear_table(view_slopes[0], positions_x, cells_x, shift_levels)
    table_y, lowest_y = shear_table(view_slopes[1], positions_y, cells_y, shift_levels)
    scale_x = float(cells_x * count_x) ** (-0.5)
    scale_y = float(cells_y * count_y) ** (-0.5)
    layered = padded_2(volume, (("pa", 0),), 1).astype(jnp.float32)
    coupling = 0.02 * (2.0 * layered[1:-1] - layered[:-2] - layered[2:])
    extended = padded_2(volume, (("gx", 1), ("gy", 2)), ghost_width)
    source_x = extended[:, ghost_width : ghost_width + cells_x, :]
    source_y = extended[:, :, ghost_width : ghost_width + cells_y]
    summands_x = jnp.einsum("vsx,pxy->vpsy", table_x, source_x, preferred_element_type=jnp.float32)
    summands_x = sheared_views(summands_x, lowest_x, ghost_width, cells_y, pad_cells)
    summands_y = jnp.einsum("vsy,pxy->vpsx", table_y, source_y, preferred_element_type=jnp.float32)
    summands_y = sheared_views(summands_y, lowest_y, ghost_width, cells_x, pad_cells)
    total_x = lax.psum(summands_x, "gx")
    total_y = lax.psum(summands_y, "gy")
    residual_x = total_x * scale_x - measured_x
    residual_y = total_y * scale_y - measured_y
    back_rx = residual_x.astype(jnp.bfloat16)
    back_ry = residual_y.astype(jnp.bfloat16)
    spread_x = spread_views(
        back_rx, lowest_x, -ghost_width, cells_y + 2 * ghost_width, pad_cells, shift_levels
    )
    spread_y = spread_views(
        back_ry, lowest_y, -ghost_width, cells_x + 2 * ghost_width, pad_cells, shift_levels
    )
    wide_x = jnp.einsum("vsx,vpsy->pxy", table_x, spread_x, preferred_element_type=jnp.float32)
    wide_y = jnp.einsum("vsy,vpsx->pxy", table_y, spread_y, preferred_element_type=jnp.float32)
    combined = jnp.pad(wide_x * scale_x, ((0, 0), (ghost_width, ghost_width), (0, 0)))
    combined = combined + jnp.pad(wide_y * scale_y, ((0, 0), (0, 0), (ghost_width, ghost_width)))
    outer = padded_2(combined.astype(jnp.bfloat16), (("gx", 1), ("gy", 2)), ghost_width).astype(
        combined.dtype
    )
    backed = combined[:, ghost_width : ghost_width + cells_x, ghost_width : ghost_width + cells_y]
    rows_band = outer[:, :, 2 * ghost_width : 2 * ghost_width + cells_y]
    columns_band = outer[:, 2 * ghost_width : 2 * ghost_width + cells_x, :]
    backed = fold_edges(backed, rows_band, ghost_width, cells_x, 1)
    backed = fold_edges(backed, columns_band, ghost_width, cells_y, 2)
    gradient = backed + coupling
    return (gradient, residual_x, residual_y)


def solution(mesh):
    return jax.shard_map(
        on_device,
        mesh=mesh,
        in_specs=(P("pa", "gx", "gy"), P(), P(None, "pa", "gy"), P(None, "pa", "gx")),
        out_specs=(P("pa", "gx", "gy"), P(None, "pa", "gy"), P(None, "pa", "gx")),
        check_vma=False,
    )
```

profile of v0, /device:TPU:9, one launch (start us, length us, event | category | flops | bytes accessed | tf_op | source)
XLA Modules:
  0.0 453.2 jit_solution(3947259791864831188)
XLA Ops:
  7.2 1.3 copy.47
  8.6 3.8 collective-permute-start
  12.4 1.9 collective-permute-start.1
  16.0 3.2 copy.52
  19.2 3.4 copy.59
  24.7 2.1 pad.56
  26.8 3.9 reshape.412
  30.7 1.9 pad.57
  32.6 2.3 copy.81
  34.9 2.2 reduce_sum.19
  37.0 5.6 %copy.58 = f32[16,2,1280]{1,0,2:T(8,128)} copy(f32[16,2,1280]{2,0,1:T(8,128)S(1)} %reduce_sum.19) | data formatting | bytes 327680 | tf_op jit(solution)/shard_map/vmap()/reduce_sum | solution.py:52
  42.6 7.8 %gather_fusion.2 = f32[16,2,512]{1,0,2:T(8,128)} fusion(f32[16,2,1280]{1,0,2:T(8,128)} %copy.58, s32[16]{0:T(128)S(1)} %get-tuple-element.41), kind=kCustom, calls=%fused_computation.2 | custom fusion | bytes 131264 | tf_op jit(solution)/shard_map/vmap()/gather | solution.py:53
  51.7 4.3 collective-permute-start.2
  56.0 1.5 collective-permute-start.3
  57.5 161.9 %all-reduce.18.cloned.1.call-done = f32[16,2,512]{1,0,2:T(8,128)} async-done(((f32[16,2,512]{1,0,2:T(8,128)}), f32[16,2,512]{1,0,2:T(8,128)}) %all-reduce.18.cloned.1.call-update) | async-done | bytes 65552 | tf_op jit(solution)/shard_map/psum | solution.py:123
  219.4 6.6 %fusion.51 = (bf16[16,2,512]{1,0,2:T(8,128)(2,1)}, f32[16,2,512]{1,0,2:T(8,128)}) fusion(f32[16,2,512]{1,0,2:T(8,128)} %copy.59, f32[16,2,512]{1,0,2:T(8,128)} %all-reduce.18.cloned.1.call-done), kind=kLoop, calls=%fused_computation.119 | loop fusion | flops 49152 | bytes 229376 | tf_op jit(solution)/shard_map/convert_element_type | solution.py:127
  225.9 2.7 copy.78
  230.7 15.0 %copy.61 = bf16[16,2,16,1024]{2,1,0,3:T(2,128)(2,1)} copy(bf16[16,2,16,1024]{3,2,0,1:T(8,128)(2,1)S(1)} %bitcast.125) | data formatting | bytes 2097152 | tf_op jit(solution)/shard_map/vmap()/reshape | solution.py:64
  245.7 21.1 %gather_fusion.3 = bf16[16,2,16,740]{2,1,3,0:T(2,128)(2,1)} fusion(bf16[16,2,16,1024]{2,1,0,3:T(2,128)(2,1)} %copy.61, s32[16]{0:T(128)S(1)} %get-tuple-element.40), kind=kCustom, calls=%fused_computation.3 | custom fusion | bytes 1515776 | tf_op jit(solution)/shard_map/vmap()/gather | solution.py:67
  266.8 8.9 %copy.62 = bf16[16,2,16,740]{3,0,2,1:T(8,128)(2,1)S(1)} copy(bf16[16,2,16,740]{2,1,3,0:T(2,128)(2,1)} %gather_fusion.3) | data formatting | bytes 1515520 | tf_op jit(solution)/shard_map/vmap()/gather | solution.py:67
  276.9 1.8 convolution_bitcast_fusion.1
  278.7 1.8 pad.52
  280.5 3.4 reshape.408
  283.9 1.7 pad.53
  285.6 2.5 copy.79
  288.1 2.0 reduce_sum.18
  290.1 6.0 %copy.51 = f32[16,2,1024]{1,0,2:T(8,128)} copy(f32[16,2,1024]{2,0,1:T(8,128)S(1)} %reduce_sum.18) | data formatting | bytes 262144 | tf_op jit(solution)/shard_map/vmap()/reduce_sum | solution.py:52
  296.1 5.1 %gather_fusion = f32[16,2,256]{1,0,2:T(8,128)} fusion(f32[16,2,1024]{1,0,2:T(8,128)} %copy.51, s32[16]{0:T(128)S(1)} %copy-done.13), kind=kCustom, calls=%fused_computation | custom fusion | bytes 65728 | tf_op jit(solution)/shard_map/vmap()/gather | solution.py:53
  301.2 58.5 %psum.14 = f32[16,2,256]{1,0,2:T(8,128)} all-reduce(f32[16,2,256]{1,0,2:T(8,128)} %gather_fusion), channel_id=1, replica_groups=mesh['gx'=8,'gy'=16,'pa'=2] {'gx'}, use_global_device_ids=true, to_apply=%region_2.3 | all-reduce | flops 8192 | bytes 65536 | tf_op jit(solution)/shard_map/psum | solution.py:122
  359.8 3.9 fusion.52
  365.8 11.2 %copy.54 = bf16[16,2,16,768]{2,1,0,3:T(2,128)(2,1)} copy(bf16[16,2,16,768]{3,2,0,1:T(8,128)(2,1)S(1)} %bitcast.127) | data formatting | bytes 1572864 | tf_op jit(solution)/shard_map/vmap()/reshape | solution.py:64
  377.0 14.9 %gather_fusion.1 = bf16[16,2,16,484]{2,1,3,0:T(2,128)(2,1)} fusion(bf16[16,2,16,768]{2,1,0,3:T(2,128)(2,1)} %copy.54, s32[16]{0:T(128)S(1)} %copy-done.8), kind=kCustom, calls=%fused_computation.1 | custom fusion | bytes 991488 | tf_op jit(solution)/shard_map/vmap()/gather | solution.py:67
  392.0 6.1 %copy.55 = bf16[16,2,16,484]{3,0,2,1:T(8,128)(2,1)S(1)} copy(bf16[16,2,16,484]{2,1,3,0:T(2,128)(2,1)} %gather_fusion.1) | data formatting | bytes 991232 | tf_op jit(solution)/shard_map/vmap()/gather | solution.py:67
  400.0 2.1 collective-permute-start.4
  402.1 3.2 collective-permute-start.5
  405.3 6.2 %collective-permute-done.5 = bf16[2,114,484]{1,2,0:T(8,128)(2,1)S(1)} collective-permute-done((bf16[2,114,484]{1,2,0:T(8,128)(2,1)S(1)}, bf16[2,114,484]{1,2,0:T(8,128)(2,1)S(1)}, u32[]{:S(2)}, u32[]{:S(2)}) %collective-permute-start.5) | collective-permute-done | bytes 220736 | tf_op jit(solution)/shard_map/ppermute | solution.py:17
  411.4 1.6 pad_maximum_fusion.10
  413.0 2.1 collective-permute-start.6
  415.1 1.3 collective-permute-start.7
  417.2 2.9 collective-permute-start.8
  420.1 1.3 collective-permute-start.9
  421.4 3.7 copy.69
  425.1 9.0 %collective-permute-done.8 = bf16[1,512,256]{1,2,0:T(8,128)(2,1)} collective-permute-done((bf16[1,512,256]{1,2,0:T(8,128)(2,1)}, bf16[1,512,256]{1,2,0:T(8,128)(2,1)}, u32[]{:S(2)}, u32[]{:S(2)}) %collective-permute-start.8) | collective-permute-done | bytes 262176 | tf_op jit(solution)/shard_map/ppermute | solution.py:16
  435.3 2.7 maximum_convert_fusion
  438.0 3.1 copy.68
  441.1 1.3 maximum_convert_fusion.3
  442.5 1.5 maximum_convert_fusion.1
  445.0 1.3 copy.67
  (96 shorter events, 15.3 us)
Async XLA Ops:
  7.2 12.0 %copy-start.21 = (f32[16,2,512]{2,1,0:T(2,128)S(1)}, f32[16,2,512]{2,1,0:T(2,128)}, u32[]{:S(2)}) copy-start(f32[16,2,512]{2,1,0:T(2,128)} %param.7) | copy-start | bytes 196612
  7.2 212.2 %all-reduce.18.cloned.1.call-start = ((), (), s32[]{:S(2)}) async-start(), calls=%async_computation | async-start | bytes 8388608 | tf_op jit(solution)/shard_map/psum | solution.py:123
  8.5 268.4 %copy-start.1 = (bf16[2,512,256]{1,2,0:T(8,128)(2,1)}, bf16[2,512,256]{1,2,0:T(8,128)(2,1)S(1)}, u32[]{:S(2)}) copy-start(bf16[2,512,256]{1,2,0:T(8,128)(2,1)S(1)} %copy.47) | copy-start | bytes 1572868
  8.6 15.5 %collective-permute-start = (bf16[2,114,256]{1,2,0:T(8,128)(2,1)S(1)}, bf16[2,114,256]{1,2,0:T(8,128)(2,1)S(1)}, u32[]{:S(2)}, u32[]{:S(2)}) collective-permute-start(bf16[2,114,256]{1,2,0:T(8,128)(2,1)S(1)} %get-tuple-element.28), channel_id=1, source_target_pairs={{0,32},{32,64},{64,96},{96,128},{128,160},{160,192},{192,224},{1,3... | collective-permute-start | bytes 350216 | tf_op jit(solution)/shard_map/ppermute | solution.py:16
  12.4 11.7 %collective-permute-start.1 = (bf16[2,114,256]{1,2,0:T(8,128)(2,1)S(1)}, bf16[2,114,256]{1,2,0:T(8,128)(2,1)S(1)}, u32[]{:S(2)}, u32[]{:S(2)}) collective-permute-start(bf16[2,114,256]{1,2,0:T(8,128)(2,1)S(1)} %get-tuple-element.29), channel_id=1, source_target_pairs={{32,0},{64,32},{96,64},{128,96},{160,128},{192,160},{224,192},{33,... | collective-permute-start | bytes 350216 | tf_op jit(solution)/shard_map/ppermute | solution.py:17
  15.4 7.2 %copy-start.18 = (bf16[16,256]{1,0:T(8,128)(2,1)}, bf16[16,256]{1,0:T(8,128)(2,1)S(1)}, u32[]{:S(2)}) copy-start(bf16[16,256]{1,0:T(8,128)(2,1)S(1)} %get-tuple-element.36) | copy-start | bytes 24580
  15.4 7.2 %copy-start.20 = (bf16[16,256]{1,0:T(8,128)(2,1)}, bf16[16,256]{1,0:T(8,128)(2,1)S(1)}, u32[]{:S(2)}) copy-start(bf16[16,256]{1,0:T(8,128)(2,1)S(1)} %get-tuple-element.37) | copy-start | bytes 24580
  15.8 6.8 %copy-start.22 = (bf16[16,512]{1,0:T(8,128)(2,1)}, bf16[16,512]{1,0:T(8,128)(2,1)S(1)}, u32[]{:S(2)}) copy-start(bf16[16,512]{1,0:T(8,128)(2,1)S(1)} %get-tuple-element.32) | copy-start | bytes 49156
  15.8 6.8 %copy-start.24 = (bf16[16,512]{1,0:T(8,128)(2,1)}, bf16[16,512]{1,0:T(8,128)(2,1)S(1)}, u32[]{:S(2)}) copy-start(bf16[16,512]{1,0:T(8,128)(2,1)S(1)} %get-tuple-element.33) | copy-start | bytes 49156
  15.9 6.7 %copy-start.14 = (s32[16,512]{1,0:T(8,128)}, s32[16,512]{1,0:T(8,128)S(1)}, u32[]{:S(2)}) copy-start(s32[16,512]{1,0:T(8,128)S(1)} %get-tuple-element.30) | copy-start | bytes 98308
  15.9 6.7 %copy-start.16 = (s32[16,512]{1,0:T(8,128)}, s32[16,512]{1,0:T(8,128)S(1)}, u32[]{:S(2)}) copy-start(s32[16,512]{1,0:T(8,128)S(1)} %get-tuple-element.31) | copy-start | bytes 98308
  24.1 26.4 %copy-start.9 = (bf16[2,114,256]{1,2,0:T(8,128)(2,1)}, bf16[2,114,256]{1,2,0:T(8,128)(2,1)S(1)}, u32[]{:S(2)}) copy-start(bf16[2,114,256]{1,2,0:T(8,128)(2,1)S(1)} %collective-permute-done) | copy-start | bytes 350212
  24.1 26.4 %copy-start.11 = (bf16[2,114,256]{1,2,0:T(8,128)(2,1)}, bf16[2,114,256]{1,2,0:T(8,128)(2,1)S(1)}, u32[]{:S(2)}) copy-start(bf16[2,114,256]{1,2,0:T(8,128)(2,1)S(1)} %collective-permute-done.1) | copy-start | bytes 350212
  51.7 225.1 %collective-permute-start.2 = (bf16[2,740,114]{1,2,0:T(8,128)(2,1)}, bf16[2,740,114]{1,2,0:T(8,128)(2,1)}, u32[]{:S(2)}, u32[]{:S(2)}) collective-permute-start(bf16[2,740,114]{1,2,0:T(8,128)(2,1)} %get-tuple-element.24), channel_id=1, source_target_pairs={{0,2},{2,4},{4,6},{6,8},{8,10},{10,12},{12,14},{14,16},{16,18},{18... | collective-permute-start | bytes 1012328 | tf_op jit(solution)/shard_map/ppermute | solution.py:16
  56.0 220.9 %collective-permute-start.3 = (bf16[2,740,114]{1,2,0:T(8,128)(2,1)S(1)}, bf16[2,740,114]{1,2,0:T(8,128)(2,1)}, u32[]{:S(2)}, u32[]{:S(2)}) collective-permute-start(bf16[2,740,114]{1,2,0:T(8,128)(2,1)S(1)} %get-tuple-element.25), channel_id=1, source_target_pairs={{2,0},{4,2},{6,4},{8,6},{10,8},{12,10},{14,12},{16,14},{18,16},{20... | collective-permute-start | bytes 1012328 | tf_op jit(solution)/shard_map/ppermute | solution.py:17
  266.8 8.9 %copy-start.19 = (bf16[16,256]{1,0:T(8,128)(2,1)S(1)}, bf16[16,256]{1,0:T(8,128)(2,1)}, u32[]{:S(2)}) copy-start(bf16[16,256]{1,0:T(8,128)(2,1)} %copy-done.18) | copy-start | bytes 24580
  275.7 1.2 copy-start.7
  275.7 1.2 copy-start.10
  275.7 1.2 copy-start.12
  290.1 6.0 %copy-start.13 = (s32[16]{0:T(128)S(1)}, s32[16]{0:T(128)}, u32[]{:S(2)}) copy-start(s32[16]{0:T(128)} %get-tuple-element.43) | copy-start | bytes 196
  365.8 11.2 %copy-start.8 = (s32[16]{0:T(128)S(1)}, s32[16]{0:T(128)}, u32[]{:S(2)}) copy-start(s32[16]{0:T(128)} %get-tuple-element.42) | copy-start | bytes 196
  392.0 6.1 %copy-start.15 = (s32[16,512]{1,0:T(8,128)S(1)}, s32[16,512]{1,0:T(8,128)}, u32[]{:S(2)}) copy-start(s32[16,512]{1,0:T(8,128)} %copy-done.14) | copy-start | bytes 98308
  392.0 6.1 %copy-start.17 = (s32[16,512]{1,0:T(8,128)S(1)}, s32[16,512]{1,0:T(8,128)}, u32[]{:S(2)}) copy-start(s32[16,512]{1,0:T(8,128)} %copy-done.16) | copy-start | bytes 98308
  392.0 6.1 %copy-start.23 = (bf16[16,512]{1,0:T(8,128)(2,1)S(1)}, bf16[16,512]{1,0:T(8,128)(2,1)}, u32[]{:S(2)}) copy-start(bf16[16,512]{1,0:T(8,128)(2,1)} %copy-done.22) | copy-start | bytes 49156
  392.0 6.1 %copy-start.25 = (bf16[16,512]{1,0:T(8,128)(2,1)S(1)}, bf16[16,512]{1,0:T(8,128)(2,1)}, u32[]{:S(2)}) copy-start(bf16[16,512]{1,0:T(8,128)(2,1)} %copy-done.24) | copy-start | bytes 49156
  398.6 1.3 copy-start.3
  399.9 16.5 %copy-start.2 = (bf16[2,512,256]{1,2,0:T(8,128)(2,1)S(1)}, bf16[2,512,256]{1,2,0:T(8,128)(2,1)}, u32[]{:S(2)}) copy-start(bf16[2,512,256]{1,2,0:T(8,128)(2,1)} %copy-done.1) | copy-start | bytes 1572868
  400.0 5.2 %collective-permute-start.4 = (bf16[2,114,484]{1,2,0:T(8,128)(2,1)S(1)}, bf16[2,114,484]{1,2,0:T(8,128)(2,1)S(1)}, u32[]{:S(2)}, u32[]{:S(2)}) collective-permute-start(bf16[2,114,484]{1,2,0:T(8,128)(2,1)S(1)} %get-tuple-element.22), channel_id=1, source_target_pairs={{0,32},{32,64},{64,96},{96,128},{128,160},{160,192},{192,224},{1,3... | collective-permute-start | bytes 662120 | tf_op jit(solution)/shard_map/ppermute | solution.py:16
  402.1 9.4 %collective-permute-start.5 = (bf16[2,114,484]{1,2,0:T(8,128)(2,1)S(1)}, bf16[2,114,484]{1,2,0:T(8,128)(2,1)S(1)}, u32[]{:S(2)}, u32[]{:S(2)}) collective-permute-start(bf16[2,114,484]{1,2,0:T(8,128)(2,1)S(1)} %get-tuple-element.23), channel_id=1, source_target_pairs={{32,0},{64,32},{96,64},{128,96},{160,128},{192,160},{224,192},{33,... | collective-permute-start | bytes 662120 | tf_op jit(solution)/shard_map/ppermute | solution.py:17
  411.4 5.8 %copy-start.5 = (bf16[2,114,484]{1,2,0:T(8,128)(2,1)}, bf16[2,114,484]{1,2,0:T(8,128)(2,1)S(1)}, u32[]{:S(2)}) copy-start(bf16[2,114,484]{1,2,0:T(8,128)(2,1)S(1)} %collective-permute-done.5) | copy-start | bytes 662116
  413.0 28.1 %collective-permute-start.6 = (bf16[2,968,114]{1,2,0:T(8,128)(2,1)}, bf16[2,968,114]{1,2,0:T(8,128)(2,1)}, u32[]{:S(2)}, u32[]{:S(2)}) collective-permute-start(bf16[2,968,114]{1,2,0:T(8,128)(2,1)} %get-tuple-element.20), channel_id=1, source_target_pairs={{0,2},{2,4},{4,6},{6,8},{8,10},{10,12},{12,14},{14,16},{16,18},{18... | collective-permute-start | bytes 1324232 | tf_op jit(solution)/shard_map/ppermute | solution.py:16
  415.1 26.0 %collective-permute-start.7 = (bf16[2,968,114]{1,2,0:T(8,128)(2,1)}, bf16[2,968,114]{1,2,0:T(8,128)(2,1)}, u32[]{:S(2)}, u32[]{:S(2)}) collective-permute-start(bf16[2,968,114]{1,2,0:T(8,128)(2,1)} %get-tuple-element.21), channel_id=1, source_target_pairs={{2,0},{4,2},{6,4},{8,6},{10,8},{12,10},{14,12},{16,14},{18,16},{20... | collective-permute-start | bytes 1324232 | tf_op jit(solution)/shard_map/ppermute | solution.py:17
  417.2 16.9 %collective-permute-start.8 = (bf16[1,512,256]{1,2,0:T(8,128)(2,1)}, bf16[1,512,256]{1,2,0:T(8,128)(2,1)}, u32[]{:S(2)}, u32[]{:S(2)}) collective-permute-start(bf16[1,512,256]{1,2,0:T(8,128)(2,1)} %get-tuple-element.26), channel_id=1, source_target_pairs={{0,1},{2,3},{4,5},{6,7},{8,9},{10,11},{12,13},{14,15},{16,17},{18,... | collective-permute-start | bytes 786440 | tf_op jit(solution)/shard_map/ppermute | solution.py:16
  420.1 15.2 %collective-permute-start.9 = (bf16[1,512,256]{1,2,0:T(8,128)(2,1)}, bf16[1,512,256]{1,2,0:T(8,128)(2,1)}, u32[]{:S(2)}, u32[]{:S(2)}) collective-permute-start(bf16[1,512,256]{1,2,0:T(8,128)(2,1)} %get-tuple-element.27), channel_id=1, source_target_pairs={{1,0},{3,2},{5,4},{7,6},{9,8},{11,10},{13,12},{15,14},{17,16},{19,... | collective-permute-start | bytes 786440 | tf_op jit(solution)/shard_map/ppermute | solution.py:17
  441.1 1.3 copy-start.6
  441.1 2.8 copy-start.4
  442.4 1.9 copy-start
Sparse Core Ops, SparseCore 0:
  50.6 168.7 all-reduce.17
where the time goes:
time: 454 us; the launch traced here: 453 us
  waiting for transfers between devices  178 us (39%)
  local copies, waits for them, and re-layouts  148 us (33%)
  blocking collectives  58.5 us (13%)
  other arithmetic  25.5 us (6%)
  starting transfers between devices  24.2 us (5%)
  between operations  14.6 us (3%)
    psum x1, waiting for transfers between devices, on_device(): total_y = lax.psum(summands_y, 'gy')  162 us
    psum x1, blocking collectives, on_device(): total_x = lax.psum(summands_x, 'gx')  58.5 us
    gather x4, local copies, waits for them, and re-layouts, spread(): lax.dynamic_slice_in_dim(skewed, leading - lowest + pad_cells, number, 2)  50.9 us
    unnamed x64, local copies, waits for them, and re-layouts  26.4 us
    reshape x2, local copies, waits for them, and re-layouts, spread(): repeated[:, :shift_levels * (row_length - 1)]  26.2 us
    ppermute x5, starting transfers between devices, padded_2(): before = lax.ppermute(last, axis, up)  15.1 us
    gather x2, local copies, waits for them, and re-layouts, shear_sum(): lax.dynamic_slice_in_dim(skewed, leading + lowest + pad_cells, number, 1)  13 us
    reduce_sum x2, local copies, waits for them, and re-layouts, shear_sum(): jnp.sum(flattened.reshape(planes, shift_levels, row_length + 1), axis=1)  11.5 us
  transfers between devices with their start and end apart: 11, of which 4 were waited for; matrix products, arithmetic and copies ran while one was open for 17% of the time, Pallas kernels for 0%

commit v1 on v0

--- a/solution.py
+++ b/solution.py
@@ -120,7 +120,7 @@
     summands_y = jnp.einsum("vsy,pxy->vpsx", table_y, source_y, preferred_element_type=jnp.float32)
     summands_y = sheared_views(summands_y, lowest_y, ghost_width, cells_x, pad_cells)
     total_x = lax.psum(summands_x, "gx")
-    total_y = lax.psum(summands_y, "gy")
+    total_y = jnp.sum(lax.all_gather(summands_y, "gy"), axis=0)
     residual_x = total_x * scale_x - measured_x
     residual_y = total_y * scale_y - measured_y
     back_rx = residual_x.astype(jnp.bfloat16)

time: 454 us -> 996 us (2.19)
  waiting for transfers between devices: 178 us -> 701 us
  other arithmetic: 25.5 us -> 45.6 us
    all_gather x0 -> x1, waiting for transfers between devices: none -> 676 us  [on_device(): total_y = jnp.sum(lax.all_gather(summands_y, 'gy'), axis=0)]
    psum x1 -> x0, waiting for transfers between devices: 162 us -> none  [on_device(): total_y = lax.psum(summands_y, 'gy')]
    reduce_sum x0 -> x1, other arithmetic: none -> 23 us  [on_device(): total_y = jnp.sum(lax.all_gather(summands_y, 'gy'), axis=0)]
    unnamed x64 -> x38, local copies, waits for them, and re-layouts: 26.4 us -> 27.1 us
  transfers between devices with their start and end apart: 11 -> 11, of which waited for: 4 -> 7; matrix products, arithmetic and copies ran while one was open for 17% -> 9% of each run, Pallas kernels for 0% -> 0%
where the time goes in v1:
time: 996 us; the launch traced here: 988 us
  waiting for transfers between devices  701 us (70%)
  local copies, waits for them, and re-layouts  145 us (15%)
  blocking collectives  49 us (5%)
  other arithmetic  45.6 us (5%)
  starting transfers between devices  28.8 us (3%)
  between operations  14.7 us (1%)
    all_gather x1, waiting for transfers between devices, on_device(): total_y = jnp.sum(lax.all_gather(summands_y, 'gy'), axis=0)  676 us
    gather x4, local copies, waits for them, and re-layouts, spread(): lax.dynamic_slice_in_dim(skewed, leading - lowest + pad_cells, number, 2)  51.2 us
    psum x1, blocking collectives, on_device(): total_x = lax.psum(summands_x, 'gx')  49 us
    unnamed x38, local copies, waits for them, and re-layouts  27.1 us
    reshape x2, local copies, waits for them, and re-layouts, spread(): repeated[:, :shift_levels * (row_length - 1)]  26.1 us
    reduce_sum x1, other arithmetic, on_device(): total_y = jnp.sum(lax.all_gather(summands_y, 'gy'), axis=0)  23 us
    ppermute x5, starting transfers between devices, padded_2(): before = lax.ppermute(last, axis, up)  20.6 us
  transfers between devices with their start and end apart: 11, of which 7 were waited for; matrix products, arithmetic and copies ran while one was open for 9% of the time, Pallas kernels for 0%

profile of v1, /device:TPU:9, one launch (start us, length us, event | category | flops | bytes accessed | tf_op | source)
XLA Modules:
  0.0 988.5 jit_solution(7381429395814740178)
XLA Ops:
  8.6 3.8 collective-permute-start
  12.4 1.9 collective-permute-start.1
  17.2 1.5 collective-permute-done.1
  20.5 2.5 reshape.412
  23.0 1.9 pad.57
  26.1 5.6 copy.53
  31.7 7.8 gather_fusion.2
  40.9 4.3 collective-permute-start.2
  45.3 1.7 collective-permute-start.3
  47.1 2.0 copy.47
  49.0 4.2 copy.54
  54.2 3.4 collective-permute-done.3
  57.6 1.9 convolution_bitcast_fusion.1
  59.5 1.8 pad.52
  61.3 3.5 reshape.408
  64.8 1.8 pad.53
  66.6 2.6 copy.74
  69.2 2.1 reduce_sum.27
  71.3 6.0 copy.46
  77.3 5.2 gather_fusion
  82.5 49.0 %psum.7 = f32[16,2,256]{1,0,2:T(8,128)} all-reduce(f32[16,2,256]{1,0,2:T(8,128)} %gather_fusion), channel_id=1, replica_groups=mesh['gx'=8,'gy'=16,'pa'=2] {'gx'}, use_global_device_ids=true, to_apply=%region_2.3 | all-reduce | flops 8192 | bytes 65536 | tf_op jit(solution)/shard_map/psum | solution.py:122
  131.5 3.6 fusion.52
  135.0 2.3 copy.72
  138.5 11.2 %copy.49 = bf16[16,2,16,768]{2,1,0,3:T(2,128)(2,1)} copy(bf16[16,2,16,768]{3,2,0,1:T(8,128)(2,1)S(1)} %bitcast.128) | data formatting | bytes 1572864 | tf_op jit(solution)/shard_map/vmap()/reshape | solution.py:64
  149.8 14.9 %gather_fusion.1 = bf16[16,2,16,484]{2,1,3,0:T(2,128)(2,1)} fusion(bf16[16,2,16,768]{2,1,0,3:T(2,128)(2,1)} %copy.49, s32[16]{0:T(128)S(1)} %get-tuple-element.42), kind=kCustom, calls=%fused_computation.1 | custom fusion | bytes 991488 | tf_op jit(solution)/shard_map/vmap()/gather | solution.py:67
  164.7 6.1 copy.50
  170.8 1.9 fusion.1
  172.8 676.2 %all-gather.3.cloned.1.call-done = f32[256,2,512]{1,0,2:T(8,128)} async-done(((f32[16,2,512]{1,0,2:T(8,128)}), f32[256,2,512]{1,0,2:T(8,128)}) %all-gather.3.cloned.1.call-update) | async-done | bytes 1048592 | tf_op jit(solution)/shard_map/all_gather | solution.py:123
  848.9 23.0 %reduce_sum.29 = f32[16,2,512]{1,0,2:T(8,128)} reduce(f32[16,16,2,512]{2,1,0,3:T(8,128)} %bitcast.22, f32[]{:T(128)} %constant.86.clone.1), dimensions={0}, to_apply=%region_5.6 | reduce | flops 245760 | bytes 1114116 | tf_op jit(solution)/shard_map/reduce_sum | solution.py:123
  872.0 6.0 fusion.51
  878.0 1.6 copy.73
  881.6 14.9 %copy.56 = bf16[16,2,16,1024]{2,1,0,3:T(2,128)(2,1)} copy(bf16[16,2,16,1024]{3,2,0,1:T(8,128)(2,1)S(1)} %bitcast.126) | data formatting | bytes 2097152 | tf_op jit(solution)/shard_map/vmap()/reshape | solution.py:64
  896.5 21.3 %gather_fusion.3 = bf16[16,2,16,740]{2,1,3,0:T(2,128)(2,1)} fusion(bf16[16,2,16,1024]{2,1,0,3:T(2,128)(2,1)} %copy.56, s32[16]{0:T(128)S(1)} %get-tuple-element.40), kind=kCustom, calls=%fused_computation.3 | custom fusion | bytes 1515776 | tf_op jit(solution)/shard_map/vmap()/gather | solution.py:67
  917.8 8.9 copy.57
  929.0 6.9 collective-permute-start.4
  936.0 1.9 collective-permute-start.5
  939.1 4.4 collective-permute-done.5
  944.2 1.5 pad_maximum_fusion.10
  945.8 3.3 collective-permute-start.6
  950.5 2.2 collective-permute-start.8
  954.0 12.2 %collective-permute-done.8 = bf16[1,512,256]{1,2,0:T(8,128)(2,1)S(1)} collective-permute-done((bf16[1,512,256]{1,2,0:T(8,128)(2,1)S(1)}, bf16[1,512,256]{1,2,0:T(8,128)(2,1)S(1)}, u32[]{:S(2)}, u32[]{:S(2)}) %collective-permute-start.8) | collective-permute-done | bytes 262176 | tf_op jit(solution)/shard_map/ppermute | solution.py:16
  966.2 1.9 collective-permute-done.9
  968.0 1.6 maximum_convert_fusion
  969.6 3.1 copy.63
  972.7 3.5 copy.64
  976.2 1.3 maximum_convert_fusion.3
  977.5 1.5 maximum_convert_fusion.1
  980.1 1.3 copy.62
  (71 shorter events, 20.7 us)
Async XLA Ops:
  7.2 841.8 %all-gather.3.cloned.1.call-start = ((), (), s32[]{:S(2)}) async-start(), calls=%async_computation | async-start | bytes 71303168 | tf_op jit(solution)/shard_map/all_gather | solution.py:123
  8.5 49.1 %copy-start.1 = (bf16[2,512,256]{1,2,0:T(8,128)(2,1)}, bf16[2,512,256]{1,2,0:T(8,128)(2,1)S(1)}, u32[]{:S(2)}) copy-start(bf16[2,512,256]{1,2,0:T(8,128)(2,1)S(1)} %copy.42) | copy-start | bytes 1572868
  8.6 8.6 collective-permute-start
  12.4 6.3 collective-permute-start.1
  18.6 0.7 copy-start.7
  39.5 0.9 copy-start.8
  40.9 13.2 %collective-permute-start.2 = (bf16[2,740,114]{1,2,0:T(8,128)(2,1)S(1)}, bf16[2,740,114]{1,2,0:T(8,128)(2,1)}, u32[]{:S(2)}, u32[]{:S(2)}) collective-permute-start(bf16[2,740,114]{1,2,0:T(8,128)(2,1)S(1)} %get-tuple-element.24), channel_id=1, source_target_pairs={{0,2},{2,4},{4,6},{6,8},{8,10},{10,12},{12,14},{14,16},{16,18},{18... | collective-permute-start | bytes 1012328 | tf_op jit(solution)/shard_map/ppermute | solution.py:16
  45.3 12.3 %collective-permute-start.3 = (bf16[2,740,114]{1,2,0:T(8,128)(2,1)S(1)}, bf16[2,740,114]{1,2,0:T(8,128)(2,1)}, u32[]{:S(2)}, u32[]{:S(2)}) collective-permute-start(bf16[2,740,114]{1,2,0:T(8,128)(2,1)S(1)} %get-tuple-element.25), channel_id=1, source_target_pairs={{2,0},{4,2},{6,4},{8,6},{10,8},{12,10},{14,12},{16,14},{18,16},{20... | collective-permute-start | bytes 1012328 | tf_op jit(solution)/shard_map/ppermute | solution.py:17
  164.7 6.1 copy-start.9
  164.7 6.1 copy-start.10
  164.7 6.1 copy-start.11
  164.7 6.1 copy-start.12
  926.7 1.6 copy-start.3
  928.9 21.5 %copy-start.2 = (bf16[2,512,256]{1,2,0:T(8,128)(2,1)S(1)}, bf16[2,512,256]{1,2,0:T(8,128)(2,1)}, u32[]{:S(2)}) copy-start(bf16[2,512,256]{1,2,0:T(8,128)(2,1)} %copy-done.1) | copy-start | bytes 1572868
  929.0 10.1 %collective-permute-start.4 = (bf16[2,114,484]{1,2,0:T(8,128)(2,1)S(1)}, bf16[2,114,484]{1,2,0:T(8,128)(2,1)S(1)}, u32[]{:S(2)}, u32[]{:S(2)}) collective-permute-start(bf16[2,114,484]{1,2,0:T(8,128)(2,1)S(1)} %get-tuple-element.22), channel_id=1, source_target_pairs={{0,32},{32,64},{64,96},{96,128},{128,160},{160,192},{192,224},{1,3... | collective-permute-start | bytes 662120 | tf_op jit(solution)/shard_map/ppermute | solution.py:16
  936.0 7.6 collective-permute-start.5
  943.5 0.7 copy-start.5
  945.8 30.4 %collective-permute-start.6 = (bf16[2,968,114]{1,2,0:T(8,128)(2,1)}, bf16[2,968,114]{1,2,0:T(8,128)(2,1)}, u32[]{:S(2)}, u32[]{:S(2)}) collective-permute-start(bf16[2,968,114]{1,2,0:T(8,128)(2,1)} %get-tuple-element.20), channel_id=1, source_target_pairs={{0,2},{2,4},{4,6},{6,8},{8,10},{10,12},{12,14},{14,16},{16,18},{18... | collective-permute-start | bytes 1324232 | tf_op jit(solution)/shard_map/ppermute | solution.py:16
  949.1 27.1 %collective-permute-start.7 = (bf16[2,968,114]{1,2,0:T(8,128)(2,1)}, bf16[2,968,114]{1,2,0:T(8,128)(2,1)}, u32[]{:S(2)}, u32[]{:S(2)}) collective-permute-start(bf16[2,968,114]{1,2,0:T(8,128)(2,1)} %get-tuple-element.21), channel_id=1, source_target_pairs={{2,0},{4,2},{6,4},{8,6},{10,8},{12,10},{14,12},{16,14},{18,16},{20... | collective-permute-start | bytes 1324232 | tf_op jit(solution)/shard_map/ppermute | solution.py:17
  950.5 15.7 %collective-permute-start.8 = (bf16[1,512,256]{1,2,0:T(8,128)(2,1)S(1)}, bf16[1,512,256]{1,2,0:T(8,128)(2,1)S(1)}, u32[]{:S(2)}, u32[]{:S(2)}) collective-permute-start(bf16[1,512,256]{1,2,0:T(8,128)(2,1)S(1)} %get-tuple-element.26), channel_id=1, source_target_pairs={{0,1},{2,3},{4,5},{6,7},{8,9},{10,11},{12,13},{14,15},{16,17},{18,... | collective-permute-start | bytes 786440 | tf_op jit(solution)/shard_map/ppermute | solution.py:16
  952.7 15.4 %collective-permute-start.9 = (bf16[1,512,256]{1,2,0:T(8,128)(2,1)S(1)}, bf16[1,512,256]{1,2,0:T(8,128)(2,1)S(1)}, u32[]{:S(2)}, u32[]{:S(2)}) collective-permute-start(bf16[1,512,256]{1,2,0:T(8,128)(2,1)S(1)} %get-tuple-element.27), channel_id=1, source_target_pairs={{1,0},{3,2},{5,4},{7,6},{9,8},{11,10},{13,12},{15,14},{17,16},{19,... | collective-permute-start | bytes 786440 | tf_op jit(solution)/shard_map/ppermute | solution.py:17
  976.2 1.3 copy-start.6
  976.2 2.8 copy-start.4
  977.5 1.9 copy-start
Sparse Core Ops, SparseCore 0:
  39.7 809.2 all-gather.2
